TPU v7x, 128 devices: a whole 4x4x4 slice. The times are simulated.
128 devices in a mesh: inst: 8 (over z_lo, x), space: 16 (over z_hi, y, core).
Axes of the slice: x: 4, y: 4, z: 4 (z_hi: 2, z_lo: 2; z = z_hi * 2 + z_lo), core: 2. Of those that a mesh axis runs over, the one named last changes fastest.
Arguments:
- field_start: float32 [32, 256, 64, 128], P('inst', 'space'), may hold values from -6 to 6
- source: float32 [32, 256, 64, 128], P('inst', 'space'), may hold values from -6 to 6
- material: int32 [256, 64, 128], P('space'), may hold values from 0 to 7
- face_flags: int32 [32, 3, 256, 64, 128], P('inst', None, 'space'), may hold values from 0 to 1
- disp_table: float32 [8], replicated, may hold values from 0.3 to 3
- perm_table: float32 [8], replicated, may hold values from 0.2 to 2
Outputs:
- residual: float32 [32, 256, 64, 128], P('inst', 'space')
- field: float32 [32, 256, 64, 128], P('inst', 'space')
All inputs are finite; a program needn't handle non-finite values.
Results may differ from a plain program's by a relative error of at most 0.00005.
Values sent between devices are 32-bit elements; how exact they have to be, the bound alone decides.
A program may use at most 128 MiB of HBM per device.

v0:
```python
import jax
import jax.numpy as jnp
from jax import lax
from jax.sharding import PartitionSpec as P

NT = 32


omega_scale = 0.25
decay_rate = 0.3
relax_weight = 0.8


def shifted(shard, axis, by):
    count = lax.axis_size(axis)
    pairs = [(i, i + by) for i in range(count) if 0 <= i + by < count]
    return lax.ppermute(shard, axis, pairs)


def with_halo(block, sides, width):
    for axis, dim in sides:
        count = lax.axis_size(axis)
        forward = [(i, i + 1) for i in range(count - 1)]
        backward = [(target, source) for source, target in forward]
        low = lax.ppermute(
            lax.slice_in_dim(block, block.shape[dim] - width, None, axis=dim), axis, forward
        )
        high = lax.ppermute(lax.slice_in_dim(block, 0, width, axis=dim), axis, backward)
        block = jnp.concatenate([low, block, high], axis=dim)
    return block


def spectral_matrix(first, count):
    rows = first + jnp.arange(count)
    cols = jnp.arange(NT)
    diff = rows[:, None] - cols[None, :]
    angle = jnp.pi * diff.astype(jnp.float32) / NT
    parity = 1.0 - 2.0 * (diff % 2).astype(jnp.float32)
    safe = jnp.where(diff == 0, 1.0, jnp.sin(angle))
    return jnp.where(diff == 0, 0.0, 0.5 * parity * jnp.cos(angle) / safe)


def lookup(material, table):
    total = jnp.zeros(material.shape, jnp.float32)
    for klass in range(table.shape[0]):
        total = total + jnp.where(material == klass, table[klass], 0.0)
    return total


def next_along(field, axis):
    count = field.shape[axis]
    zeros = jnp.zeros_like(lax.slice_in_dim(field, 0, 1, axis=axis))
    return jnp.concatenate([lax.slice_in_dim(field, 1, count, axis=axis), zeros], axis)


def prev_along(field, axis):
    count = field.shape[axis]
    zeros = jnp.zeros_like(lax.slice_in_dim(field, 0, 1, axis=axis))
    return jnp.concatenate([zeros, lax.slice_in_dim(field, 0, count - 1, axis=axis)], axis)


def face_terms(field, up_val, lo_val, kappa, lo_kappa, flow, lo_flow):
    return (
        kappa * (field - up_val)
        + lo_kappa * (field - lo_val)
        + jnp.maximum(flow, 0.0) * field
        + jnp.minimum(flow, 0.0) * up_val
        - jnp.maximum(lo_flow, 0.0) * lo_val
        - jnp.minimum(lo_flow, 0.0) * field
    )


def diag_terms(kappa, lo_kappa, flow, lo_flow):
    return kappa + lo_kappa + jnp.maximum(flow, 0.0) - jnp.minimum(lo_flow, 0.0)


def body(field_start, source, material, face_flags, disp_table, perm_table):
    count = field_start.shape[0]
    first = lax.axis_index("inst") * count
    kappa = lookup(material, disp_table)
    speed = lookup(material, perm_table)
    moments = (first + jnp.arange(count)).astype(jnp.float32)
    tide = 1.0 + 0.5 * jnp.cos(2.0 * jnp.pi * moments / NT)
    velocity = (
        speed[None, None]
        * tide[:, None, None, None, None]
        * (1.0 - 2.0 * face_flags.astype(jnp.float32))
    )
    top_plane = jnp.concatenate([kappa[-1:], velocity[:, 0, -1]], 0)
    below = shifted(top_plane, "space", 1)
    low_kappa_z = jnp.concatenate([below[:1], kappa[:-1]], 0)
    low_flow_z = jnp.concatenate([below[1:, None], velocity[:, 0, :-1]], 1)
    kappa_wide = kappa[None]
    diag = decay_rate + jnp.zeros_like(field_start)
    diag = diag + diag_terms(kappa_wide, low_kappa_z[None], velocity[:, 0], low_flow_z)
    for axis in (1, 2):
        flow = velocity[:, axis]
        diag = diag + diag_terms(
            kappa_wide, prev_along(kappa, axis)[None], flow, prev_along(flow, axis + 1)
        )
    dmat_rows = spectral_matrix(first, count)

    def coupled(field):
        piece = lax.all_gather(field, "inst", axis=0, tiled=True)
        flat = piece.reshape(piece.shape[0], -1)
        product = jnp.dot(
            dmat_rows, flat, precision=lax.Precision.HIGHEST, preferred_element_type=jnp.float32
        )
        return product.reshape(jnp.zeros(field.shape, jnp.float32).shape)

    def residual_of(field):
        padded = with_halo(field, (("space", 1),), 1)
        total = decay_rate * field
        total = total + face_terms(
            field,
            padded[:, 2:],
            padded[:, :-2],
            kappa_wide,
            low_kappa_z[None],
            velocity[:, 0],
            low_flow_z,
        )
        for axis in (1, 2):
            flow = velocity[:, axis]
            total = total + face_terms(
                field,
                next_along(field, axis + 1),
                prev_along(field, axis + 1),
                kappa_wide,
                prev_along(kappa, axis)[None],
                flow,
                prev_along(flow, axis + 1),
            )
        return omega_scale * coupled(field) + total - source

    residual = residual_of(field_start)
    middle = field_start - relax_weight * residual / diag
    second = residual_of(middle)
    field = middle - relax_weight * second / diag
    return (residual, field)


def solution(mesh):
    return jax.shard_map(
        body,
        mesh=mesh,
        in_specs=(
            P("inst", "space", None, None),
            P("inst", "space", None, None),
            P("space", None, None),
            P("inst", None, "space", None, None),
            P(),
            P(),
        ),
        out_specs=(P("inst", "space", None, None), P("inst", "space", None, None)),
        check_vma=False,
    )
```

profile of v0, /device:TPU:1, one launch (start us, length us, event | category | flops | bytes accessed | tf_op | source)
XLA Modules:
  0.0 476.9 jit_solution(4694018413515174211)
XLA Ops:
  7.2 0.0 copy-start.2
  7.2 0.0 copy-start.10
  7.2 0.0 copy-start.11
  7.2 0.0 all-gather.3.cloned.1.call-start
  7.2 0.7 all-gather.3.cloned.1.call-update
  7.9 0.0 all-gather.5.cloned.1.call-start
  8.0 0.8 copy-done.2
  8.8 0.7 fusion.80
  9.5 3.3 collective-permute-start
  12.8 3.2 collective-permute-start.2
  16.0 0.0 copy-done.10
  16.0 0.7 fusion.84
  16.7 7.8 %select_add_fusion.1 = (f32[16,64,128]{2,1,0:T(8,128)S(1)}, pred[16,64,128]{2,1,0:T(8,128)(4,1)S(1)}, pred[16,64,128]{2,1,0:T(8,128)(4,1)S(1)}, pred[16,64,128]{...) fusion(f32[]{:T(128)} %bitcast.10, f32[]{:T(128)} %bitcast.9, ...), kind=kLoop, calls=%fused_computation.68 | loop fusion | flops 3014656 | bytes 2097184 | tf_op jit(solution)/shard_map/add | solution.py:46
  24.4 0.6 slice.198
  25.1 0.0 copy-done.11
  25.1 0.7 fusion.83
  25.8 6.5 %select_add_fusion = f32[16,64,128]{2,1,0:T(8,128)S(1)} fusion(pred[16,64,128]{2,1,0:T(8,128)(4,1)} %get-tuple-element.18, pred[16,64,128]{2,1,0:T(8,128)(4,1)S(1)} %get-tuple-element.17, pred[16,64,128]{2,1,0:T(8,128)(4,1)S(1)} %get-tuple-element.16, pred[16,64,128]{2,1,0:T(8,128)(4,1)S(1)} %get-tuple-element.15, ...), kind=kLoop, calls=%fused_computation.67 | loop fusion | flops 1966080 | bytes 1572896 | tf_op jit(solution)/shard_map/add | solution.py:46
  32.3 0.3 broadcast_multiply_fusion
  32.6 0.0 copy-start.9
  32.6 4.0 fusion.6
  36.6 0.0 copy-start.1
  36.7 0.0 copy-done.9
  36.7 2.3 collective-permute-start.1
  39.0 2.4 slice_bitcast_fusion.1
  41.4 2.4 fusion.81
  43.9 2.9 fusion.82
  46.8 0.0 copy-done.1
  46.8 1.4 slice_bitcast_fusion.2
  48.2 0.0 collective-permute-done.1
  48.3 1.9 pad_maximum_fusion.5
  50.1 135.6 %all-gather.3.cloned.1.call-done = f32[32,16,64,128]{3,2,1,0:T(8,128)} async-done(((f32[4,16,64,128]{3,2,1,0:T(8,128)}), f32[32,16,64,128]{3,2,1,0:T(8,128)}) %all-gather.3.cloned.1.call-update) | async-done | bytes 16777232 | tf_op jit(solution)/shard_map/all_gather | solution.py:104
  185.7 15.2 %copy.176 = f32[4,8,1024,128]{3,1,2,0:T(8,128)S(1)} copy(f32[4,8,1024,128]{3,2,1,0:T(8,128)} %bitcast.116) | data formatting | bytes 33554432
  200.9 6.9 %copy.152 = f32[4,8,1024,128]{3,2,1,0:T(8,128)} copy(f32[4,8,1024,128]{3,1,2,0:T(8,128)S(1)} %copy.176) | data formatting | bytes 33554432
  207.8 0.0 copy-start.8
  207.8 25.3 %fusion.2 = f32[4,16,64,128]{3,0,2,1:T(4,128)} fusion(f32[16,64,128,32]{2,1,0,3:T(8,128)} %bitcast.109, s32[4]{0:T(128)S(1)} %iota_add_fusion), kind=kOutput, calls=%fused_computation.4 | convolution fusion | flops 201329536 | bytes 18874384 | tf_op jit(solution)/shard_map/dot_general | solution.py:106
  233.1 0.0 collective-permute-done
  233.1 0.0 collective-permute-done.2
  233.1 0.0 slice-done
  233.1 0.0 slice-done.1
  233.1 0.0 copy-done.3
  233.2 0.0 copy-done.5
  233.2 0.0 copy-done.8
  233.2 11.2 %divide_subtract_fusion = (f32[4,16,64,128]{3,2,1,0:T(8,128)}, f32[4,16,64,128]{3,2,1,0:T(8,128)}) fusion(f32[4,16,64,128]{3,2,1,0:T(8,128)S(1)} %copy-done.2, f32[4,16,64,127]{3,2,1,0:T(8,128)S(1)} %bitcast.114, f32[4,16,63,128]{3,2,1,0:T(8,128)S(1)} %bitcast.112, f32[4,3,16,64,128]{4,3,2,0,1:T(8,128)S(1)} %bitcast.105, ...), kind=kLoop, calls=%fused_computation.61 | loop fusion | flops 38273024 | bytes 35241984 | tf_op jit(solution)/shard_map/sub | solution.py:137
  244.4 0.0 copy-start
  244.4 0.0 all-gather.5.cloned.1.call-update
  244.4 1.6 copy-done
  246.0 0.7 fusion.79
  246.7 2.6 collective-permute-start.3
  249.3 2.9 collective-permute-start.4
  252.2 2.4 fusion.77
  254.7 2.9 fusion.78
  257.6 155.4 %all-gather.5.cloned.1.call-done = f32[32,16,64,128]{3,2,1,0:T(8,128)} async-done(((f32[4,16,64,128]{3,2,1,0:T(8,128)}), f32[32,16,64,128]{3,2,1,0:T(8,128)}) %all-gather.5.cloned.1.call-update) | async-done | bytes 16777232 | tf_op jit(solution)/shard_map/all_gather | solution.py:104
  413.0 15.2 %copy.175 = f32[4,8,1024,128]{3,1,2,0:T(8,128)S(1)} copy(f32[4,8,1024,128]{3,2,1,0:T(8,128)} %bitcast.117) | data formatting | bytes 33554432
  428.2 6.9 %copy.154 = f32[4,8,1024,128]{3,2,1,0:T(8,128)} copy(f32[4,8,1024,128]{3,1,2,0:T(8,128)S(1)} %copy.175) | data formatting | bytes 33554432
  435.1 0.0 copy-start.7
  435.1 24.9 %fusion = f32[4,16,64,128]{3,0,2,1:T(4,128)} fusion(f32[16,64,128,32]{2,1,0,3:T(8,128)} %bitcast.108, s32[4]{0:T(128)S(1)} %iota_add_fusion), kind=kOutput, calls=%fused_computation.2 | convolution fusion | flops 201329536 | bytes 18874384 | tf_op jit(solution)/shard_map/dot_general | solution.py:106
  460.0 0.0 collective-permute-done.3
  460.0 0.0 collective-permute-done.4
  460.0 0.0 slice-done.2
  460.0 0.0 slice-done.3
  460.0 0.0 copy-done.4
  460.0 0.0 copy-done.6
  460.0 0.0 copy-done.7
  460.1 9.8 %fusion.18 = f32[4,16,64,128]{3,2,1,0:T(8,128)} fusion(f32[4,16,64,128]{3,2,1,0:T(8,128)S(1)} %copy-done, f32[4,16,64,128]{3,2,1,0:T(8,128)} %param.7, f32[4,1,64,128]{3,2,1,0:T(8,128)S(1)} %collective-permute-done.4, f32[4,1,64,128]{3,2,1,0:T(8,128)S(1)} %collective-permute-done.3, f32[4,16,64,128]{3,0,2,1:T(4,128)} %fusion, ...), kind=kLoop, calls=%fused_computation.22 | loop fusion | flops 38273024 | bytes 33144832 | tf_op jit(solution)/shard_map/sub | solution.py:139
  (17 shorter events, 0.1 us)
Async XLA Ops:
  7.2 1.6 copy-start.2
  7.2 8.8 %copy-start.10 = (f32[8]{0:T(128)S(1)}, f32[8]{0:T(128)}, u32[]{:S(2)}) copy-start(f32[8]{0:T(128)} %param.10) | copy-start | bytes 100
  7.2 17.9 %copy-start.11 = (f32[8]{0:T(128)S(1)}, f32[8]{0:T(128)}, u32[]{:S(2)}) copy-start(f32[8]{0:T(128)} %param.11) | copy-start | bytes 100
  7.2 178.5 %all-gather.3.cloned.1.call-start = ((), (), s32[]{:S(2)}) async-start(), calls=%async_computation | async-start | bytes 18874368 | tf_op jit(solution)/shard_map/all_gather | solution.py:104
  7.9 405.1 %all-gather.5.cloned.1.call-start = ((), (), s32[]{:S(2)}) async-start(), calls=%async_computation.1 | async-start | bytes 18874368 | tf_op jit(solution)/shard_map/all_gather | solution.py:104
  9.5 223.7 %collective-permute-start = (f32[4,1,64,128]{3,2,1,0:T(8,128)}, f32[4,1,64,128]{3,2,1,0:T(8,128)}, u32[]{:S(2)}, u32[]{:S(2)}) collective-permute-start(f32[4,1,64,128]{3,2,1,0:T(8,128)} %get-tuple-element.27), channel_id=1, source_target_pairs={{1,0},{2,1},{3,2},{4,3},{5,4},{6,5},{7,6},{8,7},{9,8},{10,9},{11,1... | collective-permute-start | bytes 393224 | tf_op jit(solution)/shard_map/ppermute | solution.py:28
  12.8 220.3 %collective-permute-start.2 = (f32[4,1,64,128]{3,2,1,0:T(8,128)}, f32[4,1,64,128]{3,2,1,0:T(8,128)}, u32[]{:S(2)}, u32[]{:S(2)}) collective-permute-start(f32[4,1,64,128]{3,2,1,0:T(8,128)} %get-tuple-element.28), channel_id=1, source_target_pairs={{0,1},{1,2},{2,3},{3,4},{4,5},{5,6},{6,7},{7,8},{8,9},{9,10},{10,1... | collective-permute-start | bytes 393224 | tf_op jit(solution)/shard_map/ppermute | solution.py:25
  32.6 4.1 copy-start.9
  36.6 10.2 %copy-start.1 = (f32[4,3,16,64,128]{4,3,2,0,1:T(8,128)}, f32[4,3,16,64,128]{4,3,2,0,1:T(8,128)S(1)}, u32[]{:S(2)}) copy-start(f32[4,3,16,64,128]{4,3,2,0,1:T(8,128)S(1)} %fusion.6) | copy-start | bytes 18874372
  36.7 11.5 %collective-permute-start.1 = (f32[5,64,128]{2,1,0:T(8,128)S(1)}, f32[5,64,128]{2,1,0:T(8,128)S(1)}, u32[]{:S(2)}, u32[]{:S(2)}) collective-permute-start(f32[5,64,128]{2,1,0:T(8,128)S(1)} %pad_maximum_fusion.6), channel_id=1, source_target_pairs={{0,1},{1,2},{2,3},{3,4},{4,5},{5,6},{6,7},{7,8},{8,9},{9,10},{10,1... | collective-permute-start | bytes 491528 | tf_op jit(solution)/shard_map/ppermute | solution.py:17
  207.8 25.3 %slice-start = ((s8[6291456]{0:T(1024)(128)(4,1)}), s8[4194304]{0:T(1024)(128)(4,1)S(1)}, s32[]{:S(2)}) async-start(s8[6291456]{0:T(1024)(128)(4,1)} %bitcast.104), calls=%async_computation.2 | async-start | bytes 8388608
  207.8 25.3 %slice-start.1 = ((s8[6291456]{0:T(1024)(128)(4,1)}), s8[2097152]{0:T(1024)(128)(4,1)S(1)}, s32[]{:S(2)}) async-start(s8[6291456]{0:T(1024)(128)(4,1)} %bitcast.104), calls=%async_computation.3 | async-start | bytes 4194304
  207.8 25.3 %copy-start.3 = (f32[4,16,64,128]{3,2,1,0:T(8,128)S(1)}, f32[4,16,64,128]{3,2,1,0:T(8,128)}, u32[]{:S(2)}) copy-start(f32[4,16,64,128]{3,2,1,0:T(8,128)} %get-tuple-element.19) | copy-start | bytes 6291460
  207.8 25.3 %copy-start.5 = (f32[4,16,64,128]{3,2,1,0:T(8,128)S(1)}, f32[4,16,64,128]{3,2,1,0:T(8,128)}, u32[]{:S(2)}) copy-start(f32[4,16,64,128]{3,2,1,0:T(8,128)} %get-tuple-element.20) | copy-start | bytes 6291460
  207.8 25.3 %copy-start.8 = (f32[16,64,128]{2,1,0:T(8,128)S(1)}, f32[16,64,128]{2,1,0:T(8,128)}, u32[]{:S(2)}) copy-start(f32[16,64,128]{2,1,0:T(8,128)} %get-tuple-element.34) | copy-start | bytes 1572868
  244.4 1.6 copy-start
  246.7 213.3 %collective-permute-start.3 = (f32[4,1,64,128]{3,2,1,0:T(8,128)}, f32[4,1,64,128]{3,2,1,0:T(8,128)S(1)}, u32[]{:S(2)}, u32[]{:S(2)}) collective-permute-start(f32[4,1,64,128]{3,2,1,0:T(8,128)} %get-tuple-element.25), channel_id=1, source_target_pairs={{1,0},{2,1},{3,2},{4,3},{5,4},{6,5},{7,6},{8,7},{9,8},{10,9},{11,1... | collective-permute-start | bytes 393224 | tf_op jit(solution)/shard_map/ppermute | solution.py:28
  249.3 210.7 %collective-permute-start.4 = (f32[4,1,64,128]{3,2,1,0:T(8,128)}, f32[4,1,64,128]{3,2,1,0:T(8,128)S(1)}, u32[]{:S(2)}, u32[]{:S(2)}) collective-permute-start(f32[4,1,64,128]{3,2,1,0:T(8,128)} %get-tuple-element.26), channel_id=1, source_target_pairs={{0,1},{1,2},{2,3},{3,4},{4,5},{5,6},{6,7},{7,8},{8,9},{9,10},{10,1... | collective-permute-start | bytes 393224 | tf_op jit(solution)/shard_map/ppermute | solution.py:25
  435.1 24.9 %slice-start.2 = ((s8[6291456]{0:T(1024)(128)(4,1)}), s8[4194304]{0:T(1024)(128)(4,1)S(1)}, s32[]{:S(2)}) async-start(s8[6291456]{0:T(1024)(128)(4,1)} %bitcast.106), calls=%async_computation.4 | async-start | bytes 8388608
  435.1 24.9 %slice-start.3 = ((s8[6291456]{0:T(1024)(128)(4,1)}), s8[2097152]{0:T(1024)(128)(4,1)S(1)}, s32[]{:S(2)}) async-start(s8[6291456]{0:T(1024)(128)(4,1)} %bitcast.106), calls=%async_computation.5 | async-start | bytes 4194304
  435.1 25.0 %copy-start.4 = (f32[4,16,64,128]{3,2,1,0:T(8,128)S(1)}, f32[4,16,64,128]{3,2,1,0:T(8,128)}, u32[]{:S(2)}) copy-start(f32[4,16,64,128]{3,2,1,0:T(8,128)} %get-tuple-element.19) | copy-start | bytes 6291460
  435.1 25.0 %copy-start.6 = (f32[4,16,64,128]{3,2,1,0:T(8,128)S(1)}, f32[4,16,64,128]{3,2,1,0:T(8,128)}, u32[]{:S(2)}) copy-start(f32[4,16,64,128]{3,2,1,0:T(8,128)} %get-tuple-element.20) | copy-start | bytes 6291460
  435.1 25.0 %copy-start.7 = (f32[4,15,64,128]{3,2,1,0:T(8,128)S(1)}, f32[4,15,64,128]{3,2,1,0:T(8,128)}, u32[]{:S(2)}) copy-start(f32[4,15,64,128]{3,2,1,0:T(8,128)} %slice_bitcast_fusion.2) | copy-start | bytes 5898244
Sparse Core Ops, SparseCore 0:
  9.7 176.0 all-gather.2
  244.5 168.3 all-gather.4
where the time goes:
time: 484 us; the launch traced here: 477 us
  waiting for transfers between devices  292 us (60%)
  local copies, waits for them, and re-layouts  64.5 us (13%)
  matrix products  50.2 us (10%)
  other arithmetic  41.5 us (9%)
  between operations  14.6 us (3%)
  starting transfers between devices  14.4 us (3%)
    all_gather x2, waiting for transfers between devices, coupled(): piece = lax.all_gather(field, 'inst', axis=0, tiled=True)  291 us
    dot_general x2, matrix products, coupled(): jnp.dot(dmat_rows, flat, precision=lax.Precision.HIGHEST, preferred_eleme...  50.2 us
    unnamed x36, local copies, waits for them, and re-layouts  46.5 us
    add x2, other arithmetic, lookup(): total = total + jnp.where(material == klass, table[klass], 0.0)  14.2 us
    sub x1, other arithmetic, body(): middle = field_start - relax_weight * residual / diag  11.2 us
    slice x4, local copies, waits for them, and re-layouts, next_along(): lax.slice_in_dim(field, 1, count, axis=axis)  10.7 us
    sub x1, other arithmetic, body(): field = middle - relax_weight * second / diag  9.77 us
  transfers between devices with their start and end apart: 7, of which 2 were waited for; matrix products, arithmetic and copies ran while one was open for 28% of the time, Pallas kernels for 0%

commit v1 on v0

v1 whole, which is shorter than its diff:
```python
import functools
import math

import jax
import jax.numpy as jnp
from jax import lax
from jax.experimental import pallas as pl
from jax.experimental.pallas import tpu as pltpu
from jax.sharding import PartitionSpec as P

MESH = pl.DeviceIdType.MESH

NT = 32
NMAT = 8
omega_scale = 0.25
decay_rate = 0.3
relax_weight = 0.8

DEPTHS = (4, 4, 4, 4)


def spectral_row():
    row = [0.0]
    for k in range(1, NT):
        angle = math.pi * k / NT
        row.append(omega_scale * 0.5 * (-1.0) ** k * math.cos(angle) / math.sin(angle))
    row[NT // 2] = 0.0
    return row


def weighted(coefs, values):
    total = None
    for coef, value in zip(coefs, values):
        if abs(coef) < 1e-13:
            continue
        term = jnp.float32(coef) * value
        total = term if total is None else total + term
    return jnp.zeros_like(values[0]) if total is None else total


def circulant(row, values):
    n = len(values)
    if n <= 2:
        return [weighted([row[(t - s) % n] for s in range(n)], values) for t in range(n)]
    h = n // 2
    even = [values[i] + values[i + h] for i in range(h)]
    low = circulant([(row[k] + row[k + h]) / 2 for k in range(h)], even)
    odd = [values[i] - values[i + h] for i in range(h)]
    skew = [(row[k] - row[(k + h) % n]) / 2 for k in range(n)]
    first, second = [], []
    for t in range(h):
        high = weighted([skew[(t - s) % n] for s in range(h)], odd)
        first.append(low[t] + high)
        second.append(low[t] - high)
    return first + second


def kernel(
    n, nsp, disp, perm, u_in, s_in, mat_in, flag_in, res_out, fld_out,
    u, mid, src, fz, fxy, mat, kap, spd, res, idiag, pre, fwd_buf, back_buf, got, tide,
    load_sem, halo_send, halo_recv, send_sem, recv_sem, out_sem,
):
    nt, nz, nx, ny = src.shape
    rows = nx // n
    me = lax.axis_index("inst")
    sp = lax.axis_index("space")
    starts = [sum(DEPTHS[:c]) for c in range(len(DEPTHS))]
    has_below = sp > 0
    has_above = sp < nsp - 1

    def load(kind, t):
        source, target = (
            (u_in.at[t], u.at[t, pl.ds(1, nz)]),
            (flag_in.at[t, 0], fz.at[t, pl.ds(1, nz)]),
            (flag_in.at[t, pl.ds(1, 2)], fxy.at[t]),
            (s_in.at[t], src.at[t]),
        )[kind]
        return pltpu.make_async_copy(source, target, load_sem.at[kind, t])

    mat_load = pltpu.make_async_copy(mat_in, mat.at[pl.ds(1, nz)], load_sem.at[4, 0])
    for t in range(nt):
        load(0, t).start()
    mat_load.start()
    for kind in (1, 2, 3):
        for t in range(nt):
            load(kind, t).start()

    barrier = pltpu.get_barrier_semaphore()
    for r in range(1, n):
        pl.semaphore_signal(barrier, inc=1, device_id={"inst": (me + r) % n}, device_id_type=MESH)

    @pl.when(has_below)
    def _():
        pl.semaphore_signal(barrier, inc=1, device_id={"space": sp - 1}, device_id_type=MESH)

    @pl.when(has_above)
    def _():
        pl.semaphore_signal(barrier, inc=1, device_id={"space": sp + 1}, device_id_type=MESH)

    for t in range(nt):
        angles = [math.pi * 2.0 * (k * nt + t) / NT for k in range(n)]
        value = jnp.float32(0.0)
        for k in range(n):
            value = jnp.where(me == k, jnp.float32(1.0 + 0.5 * math.cos(angles[k])), value)
        tide[t] = value

    at_edge = (sp == 0) | (sp == nsp - 1)

    @pl.when(at_edge)
    def _():
        pl.semaphore_wait(barrier, n)

    @pl.when(jnp.logical_not(at_edge))
    def _():
        pl.semaphore_wait(barrier, n + 1)

    for t in range(nt):
        load(0, t).wait()

    def fwd(phase, c, r):
        field = (u, mid)[phase]
        at, depth = starts[c], DEPTHS[c]
        target = (me + r) % n
        return pltpu.make_async_remote_copy(
            src_ref=field.at[:, pl.ds(1 + at, depth), pl.ds(pl.multiple_of(target * rows, rows), rows), :],
            dst_ref=fwd_buf.at[phase, n - r, :, pl.ds(at, depth)],
            send_sem=send_sem.at[2 * phase, c, r],
            recv_sem=recv_sem.at[2 * phase, c, n - r],
            device_id={"inst": target},
            device_id_type=MESH,
        )

    def back(phase, c, r):
        at, depth = starts[c], DEPTHS[c]
        target = (me + r) % n
        return pltpu.make_async_remote_copy(
            src_ref=back_buf.at[phase, r, :, pl.ds(at, depth)],
            dst_ref=got.at[phase, :, pl.ds(at, depth), pl.ds(pl.multiple_of(me * rows, rows), rows), :],
            send_sem=send_sem.at[2 * phase + 1, c, r],
            recv_sem=recv_sem.at[2 * phase + 1, c, n - r],
            device_id={"inst": target},
            device_id_type=MESH,
        )

    def halo(which):
        up = {"space": sp + 1}
        down = {"space": sp - 1}
        source, target, where = (
            (u.at[:, nz], u.at[:, 0], up),
            (fz.at[:, nz], fz.at[:, 0], up),
            (mat.at[nz], mat.at[0], up),
            (mid.at[:, nz], mid.at[:, 0], up),
            (u.at[:, 1], u.at[:, nz + 1], down),
            (mid.at[:, 1], mid.at[:, nz + 1], down),
        )[which]
        return pltpu.make_async_remote_copy(
            src_ref=source, dst_ref=target, send_sem=halo_send.at[which], recv_sem=halo_recv.at[which],
            device_id=where, device_id_type=MESH,
        )

    def start_all(make, phase, c):
        for r in range(1, n):
            make(phase, c, r).start()

    def await_all(make, phase, c):
        for r in range(1, n):
            make(phase, c, r).wait_recv()

    start_all(fwd, 0, 0)
    start_all(fwd, 0, 1)

    mat_load.wait()
    for t in range(nt):
        load(1, t).wait()

    @pl.when(has_above)
    def _():
        for which in (0, 1, 2):
            halo(which).start()

    @pl.when(has_below)
    def _():
        halo(4).start()

    for c in range(2, len(DEPTHS)):
        start_all(fwd, 0, c)

    @pl.when(sp == 0)
    def _():
        for t in range(nt):
            u[t, 0] = jnp.zeros((nx, ny), jnp.float32)
            mid[t, 0] = jnp.zeros((nx, ny), jnp.float32)
            fz[t, 0] = jnp.zeros((nx, ny), jnp.int32)
        kap[0] = jnp.zeros((nx, ny), jnp.float32)
        spd[0] = jnp.zeros((nx, ny), jnp.float32)

    @pl.when(sp == nsp - 1)
    def _():
        for t in range(nt):
            u[t, nz + 1] = jnp.zeros((nx, ny), jnp.float32)
            mid[t, nz + 1] = jnp.zeros((nx, ny), jnp.float32)

    def look_up(z):
        classes = mat[z]
        first = jnp.full(classes.shape, disp[0], jnp.float32)
        second = jnp.full(classes.shape, perm[0], jnp.float32)
        for k in range(1, NMAT):
            hit = classes == k
            first = jnp.where(hit, disp[k], first)
            second = jnp.where(hit, perm[k], second)
        kap[z] = first
        spd[z] = second

    def layers(c, body):
        at, depth = starts[c], DEPTHS[c]

        def step(i, carry):
            body(i // depth, at + i % depth)
            return carry

        lax.fori_loop(0, nt * depth, step, 0)

    def both(flag, kappa, fast):
        hit = flag != 0
        return jnp.where(hit, fast, kappa), jnp.where(hit, kappa, fast)

    def stencil(field, t, z):
        now = field[t, z + 1]
        rate = tide[t]
        k_here = kap[z + 1]
        f_here = k_here + spd[z + 1] * rate
        k_below = kap[z]
        f_below = k_below + spd[z] * rate
        up, lo = both(fz[t, z + 1], k_here, f_here)
        up_below, lo_below = both(fz[t, z], k_below, f_below)
        total = up * field[t, z + 2] + lo_below * field[t, z]
        diag = decay_rate + lo + up_below
        for axis, size in ((0, nx), (1, ny)):
            inner = lax.broadcasted_iota(jnp.int32, (nx, ny), axis) < size - 1
            up, lo = both(fxy[t, axis, z], k_here, f_here)
            up = jnp.where(inner, up, 0.0)
            lo_in = jnp.where(inner, lo, 0.0)
            total = total + up * pltpu.roll(now, size - 1, axis)
            total = total + pltpu.roll(lo_in * now, 1, axis)
            diag = diag + lo + pltpu.roll(up, 1, axis)
        return now, total, diag

    def prepare(c):
        def body(t, z):
            now, total, diag = stencil(u, t, z)
            res[t, z] = diag * now - total - src[t, z]
            idiag[t, z] = relax_weight / diag

        layers(c, body)

    def prepare_second(c):
        def body(t, z):
            now, total, _ = stencil(mid, t, z)
            pre[t, z] = (1.0 - relax_weight) * now + idiag[t, z] * (total + src[t, z])

        layers(c, body)

    row = spectral_row()
    mine = pl.ds(pl.multiple_of(me * rows, rows), rows)

    def derive(phase, c):
        field = (u, mid)[phase]
        at, depth = starts[c], DEPTHS[c]

        def step(i, carry):
            z = at + i
            values = [field[t, z + 1, mine, :] for t in range(nt)]
            values += [fwd_buf[phase, r, t, z] for r in range(1, n) for t in range(nt)]
            sums = circulant(row, values)
            for t in range(nt):
                got[phase, t, z, mine, :] = sums[t]
            for r in range(1, n):
                for t in range(nt):
                    back_buf[phase, r, t, z] = sums[r * nt + t]
            return carry

        lax.fori_loop(0, depth, step, 0)

    def relax(c):
        def body(t, z):
            value = got[0, t, z] + res[t, z]
            res[t, z] = value
            mid[t, z + 1] = u[t, z + 1] - idiag[t, z] * value

        layers(c, body)

    def finish(c):
        def body(t, z):
            pre[t, z] = pre[t, z] - idiag[t, z] * got[1, t, z]

        layers(c, body)

    def write(which, c):
        at, depth = starts[c], DEPTHS[c]
        ref, out = ((res, res_out), (pre, fld_out))[which]
        return pltpu.make_async_copy(ref.at[:, pl.ds(at, depth)], out.at[:, pl.ds(at, depth)], out_sem.at[which, c])

    last = len(DEPTHS) - 1

    def look_up_step(i, carry):
        look_up(i + 1)
        return carry

    lax.fori_loop(0, nz, look_up_step, 0)
    for t in range(nt):
        load(2, t).wait()
        load(3, t).wait()

    def first_halo():
        @pl.when(has_below)
        def _():
            for which in (0, 1, 2):
                halo(which).wait_recv()
            look_up(0)

    def last_halo():
        @pl.when(has_above)
        def _():
            halo(4).wait_recv()

    order = (1, 2, 0, 3)
    for c in range(len(DEPTHS)):
        if order[c] == 0:
            first_halo()
        if order[c] == last:
            last_halo()
        prepare(order[c])
        await_all(fwd, 0, c)
        derive(0, c)
        start_all(back, 0, c)

    for c in range(len(DEPTHS)):
        await_all(back, 0, c)
        relax(c)
        start_all(fwd, 1, c)
        write(0, c).start()
        if c == 0:

            @pl.when(has_below)
            def _():
                halo(5).start()

        if c == last:

            @pl.when(has_above)
            def _():
                halo(3).start()

    for c in range(len(DEPTHS)):
        await_all(fwd, 1, c)
        derive(1, c)
        start_all(back, 1, c)
        if 0 < c < last:
            prepare_second(c)

    @pl.when(has_below)
    def _():
        halo(3).wait_recv()

    prepare_second(0)

    @pl.when(has_above)
    def _():
        halo(5).wait_recv()

    prepare_second(last)

    for c in range(len(DEPTHS)):
        for phase in (0, 1):
            for r in range(1, n):
                fwd(phase, c, r).wait_send()
        for r in range(1, n):
            back(0, c, r).wait_send()
        write(0, c).wait()

    @pl.when(has_above)
    def _():
        for which in (0, 1, 2, 3):
            halo(which).wait_send()

    @pl.when(has_below)
    def _():
        for which in (4, 5):
            halo(which).wait_send()

    for c in range(len(DEPTHS)):
        await_all(back, 1, c)
        finish(c)
        write(1, c).start()
    for c in range(len(DEPTHS)):
        for r in range(1, n):
            back(1, c, r).wait_send()
        write(1, c).wait()


def solution(mesh):
    n, nsp = mesh.shape["inst"], mesh.shape["space"]

    def body(field_start, source, material, face_flags, disp_table, perm_table):
        nt, nz, nx, ny = field_start.shape
        block = (nt, nz, nx, ny)
        wide = (nt, nz + 2, nx, ny)
        chunks = len(DEPTHS)
        anywhere = pl.BlockSpec(memory_space=pl.ANY)
        scalars = pl.BlockSpec(memory_space=pltpu.SMEM)
        f32 = jnp.float32
        return pl.pallas_call(
            functools.partial(kernel, n, nsp),
            out_shape=(jax.ShapeDtypeStruct(block, f32), jax.ShapeDtypeStruct(block, f32)),
            in_specs=[scalars, scalars, anywhere, anywhere, anywhere, anywhere],
            out_specs=(anywhere, anywhere),
            scratch_shapes=[
                pltpu.VMEM(wide, f32),
                pltpu.VMEM(wide, f32),
                pltpu.VMEM(block, f32),
                pltpu.VMEM((nt, nz + 1, nx, ny), jnp.int32),
                pltpu.VMEM((nt, 2, nz, nx, ny), jnp.int32),
                pltpu.VMEM((nz + 1, nx, ny), jnp.int32),
                pltpu.VMEM((nz + 1, nx, ny), f32),
                pltpu.VMEM((nz + 1, nx, ny), f32),
                pltpu.VMEM(block, f32),
                pltpu.VMEM(block, f32),
                pltpu.VMEM(block, f32),
                pltpu.VMEM((2, n, nt, nz, nx // n, ny), f32),
                pltpu.VMEM((2, n, nt, nz, nx // n, ny), f32),
                pltpu.VMEM((2, nt, nz, nx, ny), f32),
                pltpu.SMEM((nt,), f32),
                pltpu.SemaphoreType.DMA((5, nt)),
                pltpu.SemaphoreType.DMA((6,)),
                pltpu.SemaphoreType.DMA((6,)),
                pltpu.SemaphoreType.DMA((4, chunks, n)),
                pltpu.SemaphoreType.DMA((4, chunks, n)),
                pltpu.SemaphoreType.DMA((2, chunks)),
            ],
            compiler_params=pltpu.CompilerParams(
                collective_id=0, has_side_effects=True, vmem_limit_bytes=48 << 20
            ),
        )(disp_table, perm_table, field_start, source, material, face_flags)

    return jax.shard_map(
        body,
        mesh=mesh,
        in_specs=(
            P("inst", "space", None, None),
            P("inst", "space", None, None),
            P("space", None, None),
            P("inst", None, "space", None, None),
            P(),
            P(),
        ),
        out_specs=(P("inst", "space", None, None), P("inst", "space", None, None)),
        check_vma=False,
    )
```

time: 484 us -> 109 us (0.23); the launches traced: 477 us -> 109 us
  waiting for transfers between devices: 292 us -> 0 us
  Pallas kernels: 0 us -> 104 us
  local copies, waits for them, and re-layouts: 64.5 us -> 4.98 us
  matrix products: 50.2 us -> 0 us
  other arithmetic: 41.5 us -> 0 us
  starting transfers between devices: 14.4 us -> 0 us
  between operations: 14.6 us -> 0.65 us
    all_gather x2 -> x0, waiting for transfers between devices: 291 us -> none  [coupled(): piece = lax.all_gather(field, 'inst', axis=0, tiled=True)]
    pallas_call x0 -> x1, Pallas kernels: none -> 104 us  [body(): pl.pallas_call(functools.partial(kernel, n, nsp), out_shape=(jax.ShapeDty...]
    dot_general x2 -> x0, matrix products: 50.2 us -> none  [coupled(): jnp.dot(dmat_rows, flat, precision=lax.Precision.HIGHEST, preferred_eleme...]
    unnamed x36 -> x8, local copies, waits for them, and re-layouts: 46.5 us -> 4.98 us
    sub x2 -> x0, other arithmetic: 21 us -> none  [the longest x1 11.2 us: body(): middle = field_start - relax_weight * residual / diag]
    ppermute x5 -> x0, starting transfers between devices: 14.4 us -> none  [the longest x2 6.11 us: with_halo(): lax.ppermute(lax.slice_in_dim(block, block.shape[dim] - width, None, axis...]
    add x4 -> x0, other arithmetic: 14.3 us -> none  [the longest x2 14.2 us: lookup(): total = total + jnp.where(material == klass, table[klass], 0.0)]
    slice x11 -> x0, local copies, waits for them, and re-layouts: 14.1 us -> none  [the longest x4 10.7 us: next_along(): lax.slice_in_dim(field, 1, count, axis=axis)]
  transfers between devices with their start and end apart: 7 -> 0, of which waited for: 2 -> 0; matrix products, arithmetic and copies ran while one was open for 28% -> 0% of each run, Pallas kernels for 0% -> 0%
where the time goes in v1:
time: 109 us
  Pallas kernels  104 us (95%)
  local copies, waits for them, and re-layouts  4.98 us (5%)
    pallas_call x1, Pallas kernels, body(): pl.pallas_call(functools.partial(kernel, n, nsp), out_shape=(jax.ShapeDty...  104 us
    unnamed x8, local copies, waits for them, and re-layouts  4.98 us

profile of v1, /device:TPU:1, one launch (start us, length us, event | category | flops | bytes accessed | tf_op | source)
XLA Modules:
  0.0 109.3 jit_solution(14842859232250794683)
XLA Ops:
  0.6 0.0 copy-start
  0.6 1.0 copy-done
  1.7 0.0 copy-start.1
  1.7 0.7 copy-done.1
  2.3 0.0 copy-start.2
  2.3 0.7 copy-done.2
  3.0 103.7 %shard_map.77 = (f32[4,16,64,128]{3,2,1,0:T(8,128)S(1)}, f32[4,16,64,128]{3,2,1,0:T(8,128)S(1)}) custom-call(f32[8]{0:T(128)S(1)} %copy-done.1, f32[8]{0:T(128)S(1)} %copy-done.2, f32[4,16,64,128]{3,2,1,0:T(8,128)} %u_in.1, f32[4,16,64,128]{3,2,1,0:T(8,128)} %s_in.1, s32[16,64,128]{2,1,0:T(8,128)S(1)} %copy-done, s32[4,3,16,64,128]{4,3,2,1,0:T(8,128)} %flag_in.1), custom_call_target="tpu_custom_call" | custom-call | tf_op jit(solution)/shard_map/pallas_call | solution.py:412
  106.7 1.3 %copy.10 = f32[4,16,64,128]{3,2,1,0:T(8,128)} copy(f32[4,16,64,128]{3,2,1,0:T(8,128)S(1)} %get-tuple-element.4) | data formatting | bytes 4194304
  108.0 1.3 %copy.11 = f32[4,16,64,128]{3,2,1,0:T(8,128)} copy(f32[4,16,64,128]{3,2,1,0:T(8,128)S(1)} %get-tuple-element.5) | data formatting | bytes 4194304
Async XLA Ops:
  0.6 1.0 copy-start
  1.7 0.7 copy-start.1
  2.3 0.7 copy-start.2

commit v2 on v1

--- a/solution.py
+++ b/solution.py
@@ -56,9 +56,10 @@
 
 
 def kernel(
-    n, nsp, disp, perm, u_in, s_in, mat_in, flag_in, res_out, fld_out,
-    u, mid, src, fz, fxy, mat, kap, spd, res, idiag, pre, fwd_buf, back_buf, got, tide,
-    load_sem, halo_send, halo_recv, send_sem, recv_sem, out_sem,
+    n, nsp, disp_in, perm_in, u_in, s_in, mat_in, flag_in, res, pre,
+    u, mid, src, fz, fxy, mat, kap, spd, idiag, fwd_buf, back_buf, got, tide, disp, perm,
+    load_sem, halo_send, halo_recv, send_sem, recv_sem,
+    hold, hold_flag, far_send, far_recv, relay_send, relay_recv, entered,
 ):
     nt, nz, nx, ny = src.shape
     rows = nx // n
@@ -68,6 +69,14 @@
     has_below = sp > 0
     has_above = sp < nsp - 1
 
+    low, high = nsp // 2 - 1, nsp // 2
+    assert nsp == 4 * nt
+    near_below = has_below & (sp != high)
+    near_above = has_above & (sp != low)
+    is_low, is_high = sp == low, sp == high
+    up_relay = (sp > high) & (sp % 2 == 0)
+    down_relay = (sp < low - 1) & (sp % 2 == 0)
+
     def load(kind, t):
         source, target = (
             (u_in.at[t], u.at[t, pl.ds(1, nz)]),
@@ -81,6 +90,10 @@
     for t in range(nt):
         load(0, t).start()
     mat_load.start()
+    disp_load = pltpu.make_async_copy(disp_in, disp, load_sem.at[4, 1])
+    perm_load = pltpu.make_async_copy(perm_in, perm, load_sem.at[4, 2])
+    disp_load.start()
+    perm_load.start()
     for kind in (1, 2, 3):
         for t in range(nt):
             load(kind, t).start()
@@ -89,13 +102,16 @@
     for r in range(1, n):
         pl.semaphore_signal(barrier, inc=1, device_id={"inst": (me + r) % n}, device_id_type=MESH)
 
-    @pl.when(has_below)
-    def _():
-        pl.semaphore_signal(barrier, inc=1, device_id={"space": sp - 1}, device_id_type=MESH)
-
-    @pl.when(has_above)
-    def _():
-        pl.semaphore_signal(barrier, inc=1, device_id={"space": sp + 1}, device_id_type=MESH)
+    def greet(when, space):
+        @pl.when(when)
+        def _():
+            pl.semaphore_signal(barrier, inc=1, device_id={"space": space}, device_id_type=MESH)
+
+    greet(near_below, sp - 1)
+    greet(has_above, sp + 1)
+    for t in range(1, nt):
+        greet(is_low, high + 2 * t)
+    greet(down_relay, high)
 
     for t in range(nt):
         angles = [math.pi * 2.0 * (k * nt + t) / NT for k in range(n)]
@@ -104,15 +120,27 @@
             value = jnp.where(me == k, jnp.float32(1.0 + 0.5 * math.cos(angles[k])), value)
         tide[t] = value
 
-    at_edge = (sp == 0) | (sp == nsp - 1)
-
-    @pl.when(at_edge)
+    one = (sp == 0) | is_low | (sp == nsp - 1)
+
+    @pl.when(one)
     def _():
         pl.semaphore_wait(barrier, n)
 
-    @pl.when(jnp.logical_not(at_edge))
+    @pl.when(is_high)
+    def _():
+        pl.semaphore_wait(barrier, n + nt)
+
+    @pl.when(up_relay)
+    def _():
+        pl.semaphore_wait(barrier, n + 2)
+
+    @pl.when(jnp.logical_not(one | is_high | up_relay))
     def _():
         pl.semaphore_wait(barrier, n + 1)
+
+    @pl.when(is_high | up_relay)
+    def _():
+        pl.semaphore_signal(entered, inc=1, device_id={"space": low}, device_id_type=MESH)
 
     for t in range(nt):
         load(0, t).wait()
@@ -158,6 +186,77 @@
             device_id=where, device_id_type=MESH,
         )
 
+    UP, DOWN = (0, 1, 2), (3, 4)
+    slots = (0, 1, 2, 0, 2)
+
+    def planes(kind, t):
+        return (
+            (u.at[t, nz], u.at[t, 0]),
+            (fz.at[t, nz], fz.at[t, 0]),
+            (mid.at[t, nz], mid.at[t, 0]),
+            (u.at[t, 1], u.at[t, nz + 1]),
+            (mid.at[t, 1], mid.at[t, nz + 1]),
+        )[kind]
+
+    def held(kind):
+        return hold_flag if kind == 1 else hold.at[(0, 0, 1, 0, 1)[kind]]
+
+    def far(kind, t, arriving=False):
+        if kind == 5:
+            source, place, straight = mat.at[nz], mat.at[0], True
+        else:
+            source, place = planes(kind, t)
+            straight = arriving or t == (0 if kind in UP else nt - 1)
+        goal = low if kind in DOWN else high
+        return pltpu.make_async_remote_copy(
+            src_ref=source,
+            dst_ref=place if straight else held(kind),
+            send_sem=far_send.at[kind, t],
+            recv_sem=far_recv.at[kind, t] if straight else relay_recv.at[slots[kind]],
+            device_id={"space": goal if straight else (0 if kind in DOWN else high) + 2 * t},
+            device_id_type=MESH,
+        )
+
+    def relay(kind):
+        t = sp // 2 if kind in DOWN else (sp - high) // 2
+        return pltpu.make_async_remote_copy(
+            src_ref=held(kind),
+            dst_ref=planes(kind, t)[1],
+            send_sem=relay_send.at[slots[kind]],
+            recv_sem=far_recv.at[kind, t],
+            device_id={"space": low if kind in DOWN else high},
+            device_id_type=MESH,
+        )
+
+    def arrive_at_relay(kind):
+        return pltpu.make_async_remote_copy(
+            src_ref=held(kind), dst_ref=held(kind), send_sem=relay_send.at[slots[kind]],
+            recv_sem=relay_recv.at[slots[kind]], device_id={"space": low if kind in DOWN else high}, device_id_type=MESH,
+        )
+
+    def pass_on(up_kinds, down_kinds):
+        for when, kinds in ((up_relay, up_kinds), (down_relay, down_kinds)):
+
+            @pl.when(when)
+            def _():
+                for kind in kinds:
+                    arrive_at_relay(kind).wait_recv()
+                    relay(kind).start()
+
+    def far_start(when, kinds):
+        @pl.when(when)
+        def _():
+            for t in range(nt):
+                for kind in kinds:
+                    far(kind, t).start()
+
+    def far_await(when, kinds):
+        @pl.when(when)
+        def _():
+            for t in range(nt):
+                for kind in kinds:
+                    far(kind, t, True).wait_recv()
+
     def start_all(make, phase, c):
         for r in range(1, n):
             make(phase, c, r).start()
@@ -170,17 +269,21 @@
     start_all(fwd, 0, 1)
 
     mat_load.wait()
+    disp_load.wait()
+    perm_load.wait()
     for t in range(nt):
         load(1, t).wait()
 
-    @pl.when(has_above)
+    @pl.when(near_above)
     def _():
         for which in (0, 1, 2):
             halo(which).start()
 
-    @pl.when(has_below)
+    @pl.when(near_below)
     def _():
         halo(4).start()
+
+    far_start(is_high, (3,))
 
     for c in range(2, len(DEPTHS)):
         start_all(fwd, 0, c)
@@ -295,11 +398,6 @@
 
         layers(c, body)
 
-    def write(which, c):
-        at, depth = starts[c], DEPTHS[c]
-        ref, out = ((res, res_out), (pre, fld_out))[which]
-        return pltpu.make_async_copy(ref.at[:, pl.ds(at, depth)], out.at[:, pl.ds(at, depth)], out_sem.at[which, c])
-
     last = len(DEPTHS) - 1
 
     def look_up_step(i, carry):
@@ -312,61 +410,91 @@
         load(3, t).wait()
 
     def first_halo():
-        @pl.when(has_below)
+        @pl.when(near_below)
         def _():
             for which in (0, 1, 2):
                 halo(which).wait_recv()
+
+        far_await(is_high, (0, 1))
+
+        @pl.when(is_high)
+        def _():
+            far(5, 0).wait_recv()
+
+        @pl.when(has_below)
+        def _():
             look_up(0)
 
     def last_halo():
-        @pl.when(has_above)
+        @pl.when(near_above)
         def _():
             halo(4).wait_recv()
 
-    order = (1, 2, 0, 3)
+        far_await(is_low, (3,))
+
+    order = (1, 2, 0, *range(3, len(DEPTHS))) if len(DEPTHS) > 3 else (1, 0, 2)
     for c in range(len(DEPTHS)):
         if order[c] == 0:
             first_halo()
         if order[c] == last:
             last_halo()
         prepare(order[c])
+        if c == 0:
+
+            @pl.when(is_low)
+            def _():
+                pl.semaphore_wait(entered, nt)
+                far(5, 0).start()
+
+            far_start(is_low, (0, 1))
         await_all(fwd, 0, c)
         derive(0, c)
         start_all(back, 0, c)
+        if c == 0:
+            pass_on((0, 1), (3,))
 
     for c in range(len(DEPTHS)):
         await_all(back, 0, c)
         relax(c)
         start_all(fwd, 1, c)
-        write(0, c).start()
         if c == 0:
 
-            @pl.when(has_below)
+            @pl.when(near_below)
             def _():
                 halo(5).start()
 
+            far_start(is_high, (4,))
+
         if c == last:
 
-            @pl.when(has_above)
+            @pl.when(near_above)
             def _():
                 halo(3).start()
+
+            far_start(is_low, (2,))
 
     for c in range(len(DEPTHS)):
         await_all(fwd, 1, c)
         derive(1, c)
         start_all(back, 1, c)
+        if c == 2:
+            pass_on((2,), (4,))
         if 0 < c < last:
             prepare_second(c)
 
-    @pl.when(has_below)
+    @pl.when(near_below)
     def _():
         halo(3).wait_recv()
 
+    far_await(is_high, (2,))
+
     prepare_second(0)
 
-    @pl.when(has_above)
+    @pl.when(near_above)
     def _():
         halo(5).wait_recv()
+
+    far_await(is_low, (4,))
 
     prepare_second(last)
 
@@ -376,26 +504,53 @@
                 fwd(phase, c, r).wait_send()
         for r in range(1, n):
             back(0, c, r).wait_send()
-        write(0, c).wait()
-
-    @pl.when(has_above)
+
+    @pl.when(near_above)
     def _():
         for which in (0, 1, 2, 3):
             halo(which).wait_send()
 
-    @pl.when(has_below)
+    @pl.when(near_below)
     def _():
         for which in (4, 5):
             halo(which).wait_send()
+
+    for when, kinds in ((is_low, UP), (is_high, DOWN)):
+
+        @pl.when(when)
+        def _():
+            for t in range(nt):
+                for kind in kinds:
+                    far(kind, t).wait_send()
+
+    @pl.when(is_low)
+    def _():
+        far(5, 0).wait_send()
+
+    for when, kinds in ((up_relay, UP), (down_relay, DOWN)):
+
+        @pl.when(when)
+        def _():
+            for kind in kinds:
+                relay(kind).wait_send()
 
     for c in range(len(DEPTHS)):
         await_all(back, 1, c)
         finish(c)
-        write(1, c).start()
     for c in range(len(DEPTHS)):
         for r in range(1, n):
             back(1, c, r).wait_send()
-        write(1, c).wait()
+
+
+def store_kernel(res, fld, res_out, fld_out, sem):
+    copies = []
+    for t in range(res.shape[0]):
+        copies.append(pltpu.make_async_copy(res.at[t], res_out.at[t], sem.at[0, t]))
+        copies.append(pltpu.make_async_copy(fld.at[t], fld_out.at[t], sem.at[1, t]))
+    for copy in copies:
+        copy.start()
+    for copy in copies:
+        copy.wait()
 
 
 def solution(mesh):
@@ -406,14 +561,15 @@
         block = (nt, nz, nx, ny)
         wide = (nt, nz + 2, nx, ny)
         chunks = len(DEPTHS)
-        anywhere = pl.BlockSpec(memory_space=pl.ANY)
-        scalars = pl.BlockSpec(memory_space=pltpu.SMEM)
+        far = pl.BlockSpec(memory_space=pltpu.HBM)
+        near = pl.BlockSpec(memory_space=pltpu.VMEM)
         f32 = jnp.float32
-        return pl.pallas_call(
+        operands = (disp_table, perm_table, field_start, source, material, face_flags)
+        res, fld = pl.pallas_call(
             functools.partial(kernel, n, nsp),
             out_shape=(jax.ShapeDtypeStruct(block, f32), jax.ShapeDtypeStruct(block, f32)),
-            in_specs=[scalars, scalars, anywhere, anywhere, anywhere, anywhere],
-            out_specs=(anywhere, anywhere),
+            in_specs=[far] * 6,
+            out_specs=(near, near),
             scratch_shapes=[
                 pltpu.VMEM(wide, f32),
                 pltpu.VMEM(wide, f32),
@@ -424,23 +580,37 @@
                 pltpu.VMEM((nz + 1, nx, ny), f32),
                 pltpu.VMEM((nz + 1, nx, ny), f32),
                 pltpu.VMEM(block, f32),
-                pltpu.VMEM(block, f32),
-                pltpu.VMEM(block, f32),
                 pltpu.VMEM((2, n, nt, nz, nx // n, ny), f32),
                 pltpu.VMEM((2, n, nt, nz, nx // n, ny), f32),
                 pltpu.VMEM((2, nt, nz, nx, ny), f32),
                 pltpu.SMEM((nt,), f32),
+                pltpu.SMEM((NMAT,), f32),
+                pltpu.SMEM((NMAT,), f32),
                 pltpu.SemaphoreType.DMA((5, nt)),
                 pltpu.SemaphoreType.DMA((6,)),
                 pltpu.SemaphoreType.DMA((6,)),
                 pltpu.SemaphoreType.DMA((4, chunks, n)),
                 pltpu.SemaphoreType.DMA((4, chunks, n)),
-                pltpu.SemaphoreType.DMA((2, chunks)),
+                pltpu.VMEM((2, nx, ny), f32),
+                pltpu.VMEM((nx, ny), jnp.int32),
+                pltpu.SemaphoreType.DMA((6, nt)),
+                pltpu.SemaphoreType.DMA((6, nt)),
+                pltpu.SemaphoreType.DMA((3,)),
+                pltpu.SemaphoreType.DMA((3,)),
+                pltpu.SemaphoreType.REGULAR,
             ],
             compiler_params=pltpu.CompilerParams(
                 collective_id=0, has_side_effects=True, vmem_limit_bytes=48 << 20
             ),
-        )(disp_table, perm_table, field_start, source, material, face_flags)
+        )(*[pltpu.with_memory_space_constraint(a, pltpu.HBM) for a in operands])
+        return pl.pallas_call(
+            store_kernel,
+            out_shape=(jax.ShapeDtypeStruct(block, f32), jax.ShapeDtypeStruct(block, f32)),
+            in_specs=[near, near],
+            out_specs=(far, far),
+            scratch_shapes=[pltpu.SemaphoreType.DMA((2, nt))],
+            compiler_params=pltpu.CompilerParams(vmem_limit_bytes=8 << 20),
+        )(res, fld)
 
     return jax.shard_map(
         body,

time: 109 us -> 103 us (0.945)
  local copies, waits for them, and re-layouts: 4.98 us -> 0 us
  Pallas kernels: 104 us -> 102 us
    unnamed x8 -> x0, local copies, waits for them, and re-layouts: 4.98 us -> none
    pallas_call x1, Pallas kernels: 104 us -> 100 us  [body(): pl.pallas_call(functools.partial(kernel, n, nsp), out_shape=(jax.ShapeDty...]
    pallas_call x0 -> x1, Pallas kernels: none -> 2.07 us  [body(): pl.pallas_call(store_kernel, out_shape=(jax.ShapeDtypeStruct(block, f32),...]
where the time goes in v2:
time: 103 us
  Pallas kernels  102 us (99%)
    pallas_call x1, Pallas kernels, body(): pl.pallas_call(functools.partial(kernel, n, nsp), out_shape=(jax.ShapeDty...  100 us
    pallas_call x1, Pallas kernels, body(): pl.pallas_call(store_kernel, out_shape=(jax.ShapeDtypeStruct(block, f32),...  2.07 us

profile of v2, /device:TPU:1, one launch (start us, length us, event | category | flops | bytes accessed | tf_op | source)
XLA Modules:
  0.0 103.1 jit_solution(9559659945350866677)
XLA Ops:
  0.6 100.4 %shard_map.77 = (f32[4,16,64,128]{3,2,1,0:T(8,128)S(1)}, f32[4,16,64,128]{3,2,1,0:T(8,128)S(1)}) custom-call(f32[8]{0:T(128)} %disp_in.1, f32[8]{0:T(128)} %perm_in.1, f32[4,16,64,128]{3,2,1,0:T(8,128)} %u_in.1, f32[4,16,64,128]{3,2,1,0:T(8,128)} %s_in.1, s32[16,64,128]{2,1,0:T(8,128)} %mat_in.1, s32[4,3,16,64,128]{4,3,2,1,0:T(8,128)} %flag_in.1), custom_call_target="tpu_custom_call" | custom-call | tf_op jit(solution)/shard_map/pallas_call | solution.py:568
  101.0 2.1 %shard_map.78 = (f32[4,16,64,128]{3,2,1,0:T(8,128)}, f32[4,16,64,128]{3,2,1,0:T(8,128)}) custom-call(f32[4,16,64,128]{3,2,1,0:T(8,128)S(1)} %get-tuple-element.4.res, f32[4,16,64,128]{3,2,1,0:T(8,128)S(1)} %get-tuple-element.5.fld), custom_call_target="tpu_custom_call" | custom-call | tf_op jit(solution)/shard_map/pallas_call | solution.py:606

commit v3 on v2

--- a/solution.py
+++ b/solution.py
@@ -84,42 +84,44 @@
             (flag_in.at[t, pl.ds(1, 2)], fxy.at[t]),
             (s_in.at[t], src.at[t]),
         )[kind]
-        return pltpu.make_async_copy(source, target, load_sem.at[kind, t])
-
-    mat_load = pltpu.make_async_copy(mat_in, mat.at[pl.ds(1, nz)], load_sem.at[4, 0])
+        return pltpu.make_async_copy(source, target, load_sem.at[kind])
+
+    def loaded(kind):
+        source, target = (
+            (u_in, u.at[:, pl.ds(1, nz)]),
+            (flag_in.at[:, 0], fz.at[:, pl.ds(1, nz)]),
+            (flag_in.at[:, pl.ds(1, 2)], fxy),
+            (s_in, src),
+        )[kind]
+        pltpu.make_async_copy(source, target, load_sem.at[kind]).wait()
+
+    barrier = pltpu.get_barrier_semaphore()
+    for r in range(1, n):
+        pl.semaphore_signal(barrier, inc=1, device_id={"inst": (me + r) % n}, device_id_type=MESH)
+
+    def greet(when, space):
+        @pl.when(when)
+        def _():
+            pl.semaphore_signal(barrier, inc=1, device_id={"space": space}, device_id_type=MESH)
+
+    greet(near_below, sp - 1)
+    greet(has_above, sp + 1)
+    for t in range(1, nt):
+        greet(is_low, high + 2 * t)
+    greet(down_relay, high)
+
+    mat_load = pltpu.make_async_copy(mat_in, mat.at[pl.ds(1, nz)], load_sem.at[4])
     for t in range(nt):
         load(0, t).start()
     mat_load.start()
-    disp_load = pltpu.make_async_copy(disp_in, disp, load_sem.at[4, 1])
-    perm_load = pltpu.make_async_copy(perm_in, perm, load_sem.at[4, 2])
+    disp_load = pltpu.make_async_copy(disp_in, disp, load_sem.at[5])
+    perm_load = pltpu.make_async_copy(perm_in, perm, load_sem.at[6])
     disp_load.start()
     perm_load.start()
     for kind in (1, 2, 3):
         for t in range(nt):
             load(kind, t).start()
 
-    barrier = pltpu.get_barrier_semaphore()
-    for r in range(1, n):
-        pl.semaphore_signal(barrier, inc=1, device_id={"inst": (me + r) % n}, device_id_type=MESH)
-
-    def greet(when, space):
-        @pl.when(when)
-        def _():
-            pl.semaphore_signal(barrier, inc=1, device_id={"space": space}, device_id_type=MESH)
-
-    greet(near_below, sp - 1)
-    greet(has_above, sp + 1)
-    for t in range(1, nt):
-        greet(is_low, high + 2 * t)
-    greet(down_relay, high)
-
-    for t in range(nt):
-        angles = [math.pi * 2.0 * (k * nt + t) / NT for k in range(n)]
-        value = jnp.float32(0.0)
-        for k in range(n):
-            value = jnp.where(me == k, jnp.float32(1.0 + 0.5 * math.cos(angles[k])), value)
-        tide[t] = value
-
     one = (sp == 0) | is_low | (sp == nsp - 1)
 
     @pl.when(one)
@@ -142,8 +144,7 @@
     def _():
         pl.semaphore_signal(entered, inc=1, device_id={"space": low}, device_id_type=MESH)
 
-    for t in range(nt):
-        load(0, t).wait()
+    loaded(0)
 
     def fwd(phase, c, r):
         field = (u, mid)[phase]
@@ -152,8 +153,8 @@
         return pltpu.make_async_remote_copy(
             src_ref=field.at[:, pl.ds(1 + at, depth), pl.ds(pl.multiple_of(target * rows, rows), rows), :],
             dst_ref=fwd_buf.at[phase, n - r, :, pl.ds(at, depth)],
-            send_sem=send_sem.at[2 * phase, c, r],
-            recv_sem=recv_sem.at[2 * phase, c, n - r],
+            send_sem=send_sem.at[2 * phase],
+            recv_sem=recv_sem.at[2 * phase, c],
             device_id={"inst": target},
             device_id_type=MESH,
         )
@@ -164,8 +165,8 @@
         return pltpu.make_async_remote_copy(
             src_ref=back_buf.at[phase, r, :, pl.ds(at, depth)],
             dst_ref=got.at[phase, :, pl.ds(at, depth), pl.ds(pl.multiple_of(me * rows, rows), rows), :],
-            send_sem=send_sem.at[2 * phase + 1, c, r],
-            recv_sem=recv_sem.at[2 * phase + 1, c, n - r],
+            send_sem=send_sem.at[2 * phase + 1],
+            recv_sem=recv_sem.at[2 * phase + 1, c],
             device_id={"inst": target},
             device_id_type=MESH,
         )
@@ -187,7 +188,7 @@
         )
 
     UP, DOWN = (0, 1, 2), (3, 4)
-    slots = (0, 1, 2, 0, 2)
+    slots = (0, 1, 2, 0, 2, 3)
 
     def planes(kind, t):
         return (
@@ -201,18 +202,18 @@
     def held(kind):
         return hold_flag if kind == 1 else hold.at[(0, 0, 1, 0, 1)[kind]]
 
-    def far(kind, t, arriving=False):
+    def far(kind, t):
         if kind == 5:
             source, place, straight = mat.at[nz], mat.at[0], True
         else:
             source, place = planes(kind, t)
-            straight = arriving or t == (0 if kind in UP else nt - 1)
+            straight = t == (0 if kind in UP else nt - 1)
         goal = low if kind in DOWN else high
         return pltpu.make_async_remote_copy(
             src_ref=source,
             dst_ref=place if straight else held(kind),
-            send_sem=far_send.at[kind, t],
-            recv_sem=far_recv.at[kind, t] if straight else relay_recv.at[slots[kind]],
+            send_sem=far_send.at[slots[kind]],
+            recv_sem=far_recv.at[slots[kind]] if straight else relay_recv.at[slots[kind]],
             device_id={"space": goal if straight else (0 if kind in DOWN else high) + 2 * t},
             device_id_type=MESH,
         )
@@ -223,7 +224,7 @@
             src_ref=held(kind),
             dst_ref=planes(kind, t)[1],
             send_sem=relay_send.at[slots[kind]],
-            recv_sem=far_recv.at[kind, t],
+            recv_sem=far_recv.at[slots[kind]],
             device_id={"space": low if kind in DOWN else high},
             device_id_type=MESH,
         )
@@ -250,29 +251,67 @@
                 for kind in kinds:
                     far(kind, t).start()
 
+    def all_far(kind):
+        source, place = (
+            (u.at[:, nz], u.at[:, 0]),
+            (fz.at[:, nz], fz.at[:, 0]),
+            (mid.at[:, nz], mid.at[:, 0]),
+            (u.at[:, 1], u.at[:, nz + 1]),
+            (mid.at[:, 1], mid.at[:, nz + 1]),
+        )[kind]
+        return pltpu.make_async_remote_copy(
+            src_ref=source, dst_ref=place, send_sem=far_send.at[slots[kind]], recv_sem=far_recv.at[slots[kind]],
+            device_id={"space": low if kind in DOWN else high}, device_id_type=MESH,
+        )
+
     def far_await(when, kinds):
         @pl.when(when)
         def _():
-            for t in range(nt):
-                for kind in kinds:
-                    far(kind, t, True).wait_recv()
+            for kind in kinds:
+                all_far(kind).wait_recv()
 
     def start_all(make, phase, c):
-        for r in range(1, n):
+        def step(r, carry):
             make(phase, c, r).start()
-
-    def await_all(make, phase, c):
-        for r in range(1, n):
-            make(phase, c, r).wait_recv()
+            return carry
+
+        lax.fori_loop(1, n, step, 0)
+
+    def whole(leg, phase, c, ref):
+        return pltpu.make_async_remote_copy(
+            src_ref=ref,
+            dst_ref=ref,
+            send_sem=send_sem.at[2 * phase + leg],
+            recv_sem=recv_sem.at[2 * phase + leg, c],
+            device_id={"inst": (me + 1) % n},
+            device_id_type=MESH,
+        )
+
+    def await_fwd(phase, c):
+        ref = fwd_buf.at[phase, pl.ds(1, n - 1), :, pl.ds(starts[c], DEPTHS[c])]
+        whole(0, phase, c, ref).wait_recv()
+
+    def await_back(phase, c):
+        ref = got.at[phase, :, pl.ds(starts[c], DEPTHS[c]), pl.ds(0, (n - 1) * rows), :]
+        whole(1, phase, c, ref).wait_recv()
+
+    def await_sent(leg, phase):
+        whole(leg, phase, 0, (fwd_buf, back_buf)[leg].at[phase, pl.ds(1, n - 1)]).wait_send()
 
     start_all(fwd, 0, 0)
     start_all(fwd, 0, 1)
+
+    for t in range(nt):
+        angles = [math.pi * 2.0 * (k * nt + t) / NT for k in range(n)]
+        value = jnp.float32(0.0)
+        for k in range(n):
+            value = jnp.where(me == k, jnp.float32(1.0 + 0.5 * math.cos(angles[k])), value)
+        tide[t] = value
 
     mat_load.wait()
     disp_load.wait()
     perm_load.wait()
-    for t in range(nt):
-        load(1, t).wait()
+    loaded(1)
 
     @pl.when(near_above)
     def _():
@@ -405,9 +444,8 @@
         return carry
 
     lax.fori_loop(0, nz, look_up_step, 0)
-    for t in range(nt):
-        load(2, t).wait()
-        load(3, t).wait()
+    loaded(2)
+    loaded(3)
 
     def first_halo():
         @pl.when(near_below)
@@ -447,14 +485,14 @@
                 far(5, 0).start()
 
             far_start(is_low, (0, 1))
-        await_all(fwd, 0, c)
+        await_fwd(0, c)
         derive(0, c)
         start_all(back, 0, c)
         if c == 0:
             pass_on((0, 1), (3,))
 
     for c in range(len(DEPTHS)):
-        await_all(back, 0, c)
+        await_back(0, c)
         relax(c)
         start_all(fwd, 1, c)
         if c == 0:
@@ -474,7 +512,7 @@
             far_start(is_low, (2,))
 
     for c in range(len(DEPTHS)):
-        await_all(fwd, 1, c)
+        await_fwd(1, c)
         derive(1, c)
         start_all(back, 1, c)
         if c == 2:
@@ -498,12 +536,9 @@
 
     prepare_second(last)
 
-    for c in range(len(DEPTHS)):
-        for phase in (0, 1):
-            for r in range(1, n):
-                fwd(phase, c, r).wait_send()
-        for r in range(1, n):
-            back(0, c, r).wait_send()
+    await_sent(0, 0)
+    await_sent(1, 0)
+    await_sent(0, 1)
 
     @pl.when(near_above)
     def _():
@@ -519,9 +554,8 @@
 
         @pl.when(when)
         def _():
-            for t in range(nt):
-                for kind in kinds:
-                    far(kind, t).wait_send()
+            for kind in kinds:
+                all_far(kind).wait_send()
 
     @pl.when(is_low)
     def _():
@@ -535,11 +569,9 @@
                 relay(kind).wait_send()
 
     for c in range(len(DEPTHS)):
-        await_all(back, 1, c)
+        await_back(1, c)
         finish(c)
-    for c in range(len(DEPTHS)):
-        for r in range(1, n):
-            back(1, c, r).wait_send()
+    await_sent(1, 1)
 
 
 def store_kernel(res, fld, res_out, fld_out, sem):
@@ -586,15 +618,15 @@
                 pltpu.SMEM((nt,), f32),
                 pltpu.SMEM((NMAT,), f32),
                 pltpu.SMEM((NMAT,), f32),
-                pltpu.SemaphoreType.DMA((5, nt)),
+                pltpu.SemaphoreType.DMA((7,)),
                 pltpu.SemaphoreType.DMA((6,)),
                 pltpu.SemaphoreType.DMA((6,)),
-                pltpu.SemaphoreType.DMA((4, chunks, n)),
-                pltpu.SemaphoreType.DMA((4, chunks, n)),
+                pltpu.SemaphoreType.DMA((4,)),
+                pltpu.SemaphoreType.DMA((4, chunks)),
                 pltpu.VMEM((2, nx, ny), f32),
                 pltpu.VMEM((nx, ny), jnp.int32),
-                pltpu.SemaphoreType.DMA((6, nt)),
-                pltpu.SemaphoreType.DMA((6, nt)),
+                pltpu.SemaphoreType.DMA((4,)),
+                pltpu.SemaphoreType.DMA((4,)),
                 pltpu.SemaphoreType.DMA((3,)),
                 pltpu.SemaphoreType.DMA((3,)),
                 pltpu.SemaphoreType.REGULAR,

time: 103 us -> 101 us (0.981)
  Pallas kernels: 102 us -> 99.8 us
    pallas_call x1, Pallas kernels: 100 us -> 97.7 us  [body(): pl.pallas_call(functools.partial(kernel, n, nsp), out_shape=(jax.ShapeDty...]
where the time goes in v3:
time: 101 us; the launch traced here: 100 us
  Pallas kernels  99.8 us (99%)
    pallas_call x1, Pallas kernels, body(): pl.pallas_call(functools.partial(kernel, n, nsp), out_shape=(jax.ShapeDty...  97.7 us
    pallas_call x1, Pallas kernels, body(): pl.pallas_call(store_kernel, out_shape=(jax.ShapeDtypeStruct(block, f32),...  2.07 us

profile of v3, /device:TPU:1, one launch (start us, length us, event | category | flops | bytes accessed | tf_op | source)
XLA Modules:
  0.0 100.4 jit_solution(8203050697319782691)
XLA Ops:
  0.6 97.7 %shard_map.77 = (f32[4,16,64,128]{3,2,1,0:T(8,128)S(1)}, f32[4,16,64,128]{3,2,1,0:T(8,128)S(1)}) custom-call(f32[8]{0:T(128)} %disp_in.1, f32[8]{0:T(128)} %perm_in.1, f32[4,16,64,128]{3,2,1,0:T(8,128)} %u_in.1, f32[4,16,64,128]{3,2,1,0:T(8,128)} %s_in.1, s32[16,64,128]{2,1,0:T(8,128)} %mat_in.1, s32[4,3,16,64,128]{4,3,2,1,0:T(8,128)} %flag_in.1), custom_call_target="tpu_custom_call" | custom-call | tf_op jit(solution)/shard_map/pallas_call | solution.py:600
  98.4 2.1 %shard_map.78 = (f32[4,16,64,128]{3,2,1,0:T(8,128)}, f32[4,16,64,128]{3,2,1,0:T(8,128)}) custom-call(f32[4,16,64,128]{3,2,1,0:T(8,128)S(1)} %get-tuple-element.4.res, f32[4,16,64,128]{3,2,1,0:T(8,128)S(1)} %get-tuple-element.5.fld), custom_call_target="tpu_custom_call" | custom-call | tf_op jit(solution)/shard_map/pallas_call | solution.py:638

commit v4 on v3

--- a/solution.py
+++ b/solution.py
@@ -16,7 +16,7 @@
 decay_rate = 0.3
 relax_weight = 0.8
 
-DEPTHS = (4, 4, 4, 4)
+DEPTHS = (5, 5, 4, 2)
 
 
 def spectral_row():

time: 101 us -> 100 us (0.990)
    pallas_call x1, Pallas kernels: 97.7 us -> 96.7 us  [body(): pl.pallas_call(functools.partial(kernel, n, nsp), out_shape=(jax.ShapeDty...]
where the time goes in v4:
time: 100 us; the launch traced here: 99.4 us
  Pallas kernels  98.8 us (99%)
    pallas_call x1, Pallas kernels, body(): pl.pallas_call(functools.partial(kernel, n, nsp), out_shape=(jax.ShapeDty...  96.7 us
    pallas_call x1, Pallas kernels, body(): pl.pallas_call(store_kernel, out_shape=(jax.ShapeDtypeStruct(block, f32),...  2.07 us

profile of v4, /device:TPU:1, one launch (start us, length us, event | category | flops | bytes accessed | tf_op | source)
XLA Modules:
  0.0 99.4 jit_solution(8031634005104610452)
XLA Ops:
  0.6 96.7 %shard_map.77 = (f32[4,16,64,128]{3,2,1,0:T(8,128)S(1)}, f32[4,16,64,128]{3,2,1,0:T(8,128)S(1)}) custom-call(f32[8]{0:T(128)} %disp_in.1, f32[8]{0:T(128)} %perm_in.1, f32[4,16,64,128]{3,2,1,0:T(8,128)} %u_in.1, f32[4,16,64,128]{3,2,1,0:T(8,128)} %s_in.1, s32[16,64,128]{2,1,0:T(8,128)} %mat_in.1, s32[4,3,16,64,128]{4,3,2,1,0:T(8,128)} %flag_in.1), custom_call_target="tpu_custom_call" | custom-call | tf_op jit(solution)/shard_map/pallas_call | solution.py:600
  97.4 2.1 %shard_map.78 = (f32[4,16,64,128]{3,2,1,0:T(8,128)}, f32[4,16,64,128]{3,2,1,0:T(8,128)}) custom-call(f32[4,16,64,128]{3,2,1,0:T(8,128)S(1)} %get-tuple-element.4.res, f32[4,16,64,128]{3,2,1,0:T(8,128)S(1)} %get-tuple-element.5.fld), custom_call_target="tpu_custom_call" | custom-call | tf_op jit(solution)/shard_map/pallas_call | solution.py:638

commit v5 on v4

--- a/solution.py
+++ b/solution.py
@@ -16,7 +16,7 @@
 decay_rate = 0.3
 relax_weight = 0.8
 
-DEPTHS = (5, 5, 4, 2)
+DEPTHS = (5, 5, 5, 1)
 
 
 def spectral_row():
@@ -575,14 +575,11 @@
 
 
 def store_kernel(res, fld, res_out, fld_out, sem):
-    copies = []
     for t in range(res.shape[0]):
-        copies.append(pltpu.make_async_copy(res.at[t], res_out.at[t], sem.at[0, t]))
-        copies.append(pltpu.make_async_copy(fld.at[t], fld_out.at[t], sem.at[1, t]))
-    for copy in copies:
-        copy.start()
-    for copy in copies:
-        copy.wait()
+        pltpu.make_async_copy(res.at[t], res_out.at[t], sem.at[0]).start()
+        pltpu.make_async_copy(fld.at[t], fld_out.at[t], sem.at[1]).start()
+    pltpu.make_async_copy(res, res_out, sem.at[0]).wait()
+    pltpu.make_async_copy(fld, fld_out, sem.at[1]).wait()
 
 
 def solution(mesh):
@@ -640,7 +637,7 @@
             out_shape=(jax.ShapeDtypeStruct(block, f32), jax.ShapeDtypeStruct(block, f32)),
             in_specs=[near, near],
             out_specs=(far, far),
-            scratch_shapes=[pltpu.SemaphoreType.DMA((2, nt))],
+            scratch_shapes=[pltpu.SemaphoreType.DMA((2,))],
             compiler_params=pltpu.CompilerParams(vmem_limit_bytes=8 << 20),
         )(res, fld)
 

time: 100 us -> 100 us (level)
  no operation moved by 1% of the time
where the time goes in v5:
time: 100 us; the launch traced here: 99.8 us
  Pallas kernels  99.2 us (99%)
    pallas_call x1, Pallas kernels, body(): pl.pallas_call(functools.partial(kernel, n, nsp), out_shape=(jax.ShapeDty...  97.1 us
    pallas_call x1, Pallas kernels, body(): pl.pallas_call(store_kernel, out_shape=(jax.ShapeDtypeStruct(block, f32),...  2.02 us

profile of v5, /device:TPU:1, one launch (start us, length us, event | category | flops | bytes accessed | tf_op | source)
XLA Modules:
  0.0 99.8 jit_solution(10813479041047106162)
XLA Ops:
  0.6 97.1 %shard_map.77 = (f32[4,16,64,128]{3,2,1,0:T(8,128)S(1)}, f32[4,16,64,128]{3,2,1,0:T(8,128)S(1)}) custom-call(f32[8]{0:T(128)} %disp_in.1, f32[8]{0:T(128)} %perm_in.1, f32[4,16,64,128]{3,2,1,0:T(8,128)} %u_in.1, f32[4,16,64,128]{3,2,1,0:T(8,128)} %s_in.1, s32[16,64,128]{2,1,0:T(8,128)} %mat_in.1, s32[4,3,16,64,128]{4,3,2,1,0:T(8,128)} %flag_in.1), custom_call_target="tpu_custom_call" | custom-call | tf_op jit(solution)/shard_map/pallas_call | solution.py:597
  97.8 2.0 %shard_map.78 = (f32[4,16,64,128]{3,2,1,0:T(8,128)}, f32[4,16,64,128]{3,2,1,0:T(8,128)}) custom-call(f32[4,16,64,128]{3,2,1,0:T(8,128)S(1)} %get-tuple-element.4.res, f32[4,16,64,128]{3,2,1,0:T(8,128)S(1)} %get-tuple-element.5.fld), custom_call_target="tpu_custom_call" | custom-call | tf_op jit(solution)/shard_map/pallas_call | solution.py:635
